TPU v7x, 32 devices: a whole 2x2x4 slice. The times are simulated.
32 devices in a mesh: grp: 2 (over y), gx: 4 (over z), gy: 4 (over x, core).
Axes of the slice: x: 2, y: 2, z: 4, core: 2. Of those that a mesh axis runs over, the one named last changes fastest.
Arguments:
- input_activation: bfloat16 [32, 32, 1024], P(('grp', 'gx'), 'gy'), parts along dimension 0, may hold values from -6 to 6
- pre_one: bfloat16 [32, 32, 1024], P(('grp', 'gx'), 'gy'), parts along dimension 0, may hold values from -6 to 6
- pre_two: bfloat16 [32, 32, 1024], P(('grp', 'gx'), 'gy'), parts along dimension 0, may hold values from -6 to 6
- w_one: bfloat16 [27, 64, 64], replicated, may hold values from -0.15625 to 0.15625
- w_two: bfloat16 [27, 64, 64], replicated, may hold values from -0.15625 to 0.15625
- w_trans: bfloat16 [512, 512], replicated, may hold values from -0.5 to 0.5
- keep_mask: int32 [8, 8], replicated, may hold values 0 or 1
- out_grad: bfloat16 [16, 16, 8, 512], P('grp', 'gy', None, 'gx'), parts along dimension 0, may hold values from -6 to 6
Outputs:
- grad_in: bfloat16 [32, 32, 1024], P(('grp', 'gx'), 'gy'), parts along dimension 0
- grad_w_one: float32 [54, 64, 64], P('grp'), parts along dimension 0
- grad_w_two: float32 [54, 64, 64], P('grp'), parts along dimension 0
- grad_w_trans: float32 [1024, 512], P('grp'), parts along dimension 0
There are 2 independent parts, one for each index of `grp`. A program takes and returns all parts, laid end to end along the dimension named above; an argument that names none is the same for every part. Nothing has to cross between parts.
All inputs are finite; a program needn't handle non-finite values.
Results may differ from a plain program's by a relative error of at most 0.0058.
Values may be sent and summed in bfloat16 or wider, within the bound.
No kernel may reach another device: no remote copies, remote signals or barrier semaphores. Data moves between devices by JAX's collectives and lax.ppermute only.
A program may use at most 64 MiB of HBM per device.

v0:
```python
import math
import jax
import jax.numpy as jnp
from jax import lax
from jax.sharding import PartitionSpec as P

DILATION_STEP = 2


def padded(cells, sides, width):
    for axis, dim in sides:
        count = lax.axis_size(axis)
        ends = count - 1
        head = lax.slice_in_dim(cells, 0, width, axis=dim)
        tail = lax.slice_in_dim(cells, cells.shape[dim] - width, cells.shape[dim], axis=dim)
        cells = jnp.concatenate(
            [
                lax.ppermute(tail, axis, [(i, (i + 1) % count) for i in range(ends)]),
                cells,
                lax.ppermute(head, axis, [((i + 1) % count, i) for i in range(ends)]),
            ],
            axis=dim,
        )
    return cells


def split_layout(joined_layout, channel_count):
    return joined_layout.reshape(joined_layout.shape[0], joined_layout.shape[1], -1, channel_count)


def to_blocks(cube_volume):
    shape_all = cube_volume.shape
    parted = cube_volume.reshape(
        shape_all[0] // 2, 2, shape_all[1] // 2, 2, shape_all[2] // 2, 2, shape_all[3]
    )
    parted = parted.transpose(0, 2, 4, 1, 3, 5, 6)
    return parted.reshape(shape_all[0] // 2, shape_all[1] // 2, shape_all[2] // 2, 8 * shape_all[3])


def from_blocks(blocked, channel_count):
    shape_all = blocked.shape
    parted = blocked.reshape(shape_all[0], shape_all[1], shape_all[2], 2, 2, 2, channel_count)
    parted = parted.transpose(0, 3, 1, 4, 2, 5, 6)
    return parted.reshape(2 * shape_all[0], 2 * shape_all[1], 2 * shape_all[2], channel_count)


def padding_depth(cube_volume, margin):
    return jnp.pad(cube_volume, ((0, 0), (0, 0), (margin, margin), (0, 0)))


def weight_terms(bordered_input, upstream_gradient):
    channel_count = upstream_gradient.shape[3]
    grid_extent = upstream_gradient.shape
    padded_input = padding_depth(bordered_input, DILATION_STEP)
    flat_grad = upstream_gradient.reshape(-1, channel_count)
    partials = []
    for x_index in range(3):
        for y_index in range(3):
            sliding_window = padded_input[
                DILATION_STEP * x_index : DILATION_STEP * x_index + grid_extent[0],
                DILATION_STEP * y_index : DILATION_STEP * y_index + grid_extent[1],
            ]
            columns = jnp.concatenate(
                [
                    sliding_window[
                        :, :, DILATION_STEP * tap_index : DILATION_STEP * tap_index + grid_extent[2]
                    ].reshape(-1, channel_count)
                    for tap_index in range(3)
                ],
                axis=1,
            )
            partials.append(
                lax.dot_general(
                    columns, flat_grad, (((0,), (0,)), ((), ())), preferred_element_type=jnp.float32
                )
            )
    return jnp.stack(partials).reshape(27, channel_count, channel_count)


def data_terms(bordered_input, weights):
    channel_count = weights.shape[1]
    x_stretch = bordered_input.shape[0] - 2 * DILATION_STEP
    y_stretch = bordered_input.shape[1] - 2 * DILATION_STEP
    depth_cells = bordered_input.shape[2]
    padded_input = padding_depth(bordered_input, DILATION_STEP)
    stacked = jnp.transpose(weights, (0, 2, 1)).reshape(9, 3 * channel_count, channel_count)
    running = jnp.zeros((x_stretch * y_stretch * depth_cells, channel_count), jnp.float32)
    for x_index in range(3):
        for y_index in range(3):
            sliding_window = padded_input[
                DILATION_STEP * (2 - x_index) : DILATION_STEP * (2 - x_index) + x_stretch,
                DILATION_STEP * (2 - y_index) : DILATION_STEP * (2 - y_index) + y_stretch,
            ]
            columns = jnp.concatenate(
                [
                    sliding_window[
                        :,
                        :,
                        DILATION_STEP * (2 - tap_index) : DILATION_STEP * (2 - tap_index)
                        + depth_cells,
                    ].reshape(-1, channel_count)
                    for tap_index in range(3)
                ],
                axis=1,
            )
            running = running + jnp.dot(
                columns, stacked[x_index * 3 + y_index], preferred_element_type=jnp.float32
            )
    return running.reshape(x_stretch, y_stretch, depth_cells, channel_count)


def body(input_activation, pre_one, pre_two, w_one, w_two, w_trans, keep_mask, out_grad):
    channel_count = w_one.shape[1]
    x_stretch, y_stretch, joined_layout = input_activation.shape
    depth_cells = joined_layout // channel_count
    width_t = w_trans.shape[0]
    factor = 1.0 / math.sqrt(
        x_stretch * lax.axis_size("gx") * y_stretch * lax.axis_size("gy") * depth_cells
    )
    blocks = jnp.repeat(
        jnp.repeat(keep_mask.astype(jnp.bfloat16), channel_count, axis=0), channel_count, axis=1
    )
    w_kept = w_trans * blocks
    regrouped = lax.all_to_all(out_grad, "gx", split_axis=0, concat_axis=3, tiled=True)
    grad_rows = regrouped.reshape(-1, width_t)
    back_blocks = lax.dot_general(
        grad_rows, w_kept, (((1,), (1,)), ((), ())), preferred_element_type=jnp.float32
    ).astype(jnp.bfloat16)
    act_two = split_layout(jnp.maximum(pre_two, 0), channel_count)
    two_rows = to_blocks(act_two).reshape(-1, width_t)
    trans_term = (
        lax.dot_general(
            two_rows, grad_rows, (((0,), (0,)), ((), ())), preferred_element_type=jnp.float32
        )
        * blocks.astype(jnp.float32)
        * factor
    )
    grad_w_trans = lax.psum(trans_term, ("gx", "gy"))
    back_two = from_blocks(
        back_blocks.reshape(x_stretch // 2, y_stretch // 2, depth_cells // 2, width_t),
        channel_count,
    )
    back_two = jnp.where(
        split_layout(pre_two, channel_count) > 0, back_two, jnp.zeros_like(back_two)
    )
    first_activation = jnp.maximum(pre_one, 0)
    bordered_input = padded(
        jnp.concatenate([input_activation, first_activation], axis=2),
        (("gx", 0), ("gy", 1)),
        DILATION_STEP,
    )
    in_rim = split_layout(bordered_input[:, :, :joined_layout], channel_count)
    one_rim = split_layout(bordered_input[:, :, joined_layout:], channel_count)
    two_term = weight_terms(one_rim, back_two) * factor
    flattened_backward = back_two.reshape(x_stretch, y_stretch, joined_layout)
    narrowed_slice = split_layout(
        padded(flattened_backward, (("gx", 0), ("gy", 1)), DILATION_STEP), channel_count
    )
    first_backward = data_terms(narrowed_slice, w_two)
    first_backward = jnp.where(
        split_layout(pre_one, channel_count) > 0, first_backward, jnp.zeros_like(first_backward)
    ).astype(jnp.bfloat16)
    one_grad_rim = split_layout(
        padded(
            first_backward.reshape(x_stretch, y_stretch, joined_layout),
            (("gx", 0), ("gy", 1)),
            DILATION_STEP,
        ),
        channel_count,
    )
    grad_w_two = lax.psum(two_term, ("gx", "gy"))
    one_term = weight_terms(in_rim, first_backward) * factor
    grad_w_one = lax.psum(one_term, ("gx", "gy"))
    grad_in = (
        data_terms(one_grad_rim, w_one)
        .astype(jnp.bfloat16)
        .reshape(x_stretch, y_stretch, joined_layout)
    )
    return (grad_in, grad_w_one, grad_w_two, grad_w_trans)


def solution(mesh):
    return jax.shard_map(
        body,
        mesh=mesh,
        in_specs=(
            P(("grp", "gx"), "gy", None),
            P(("grp", "gx"), "gy", None),
            P(("grp", "gx"), "gy", None),
            P(),
            P(),
            P(),
            P(),
            P("grp", "gy", None, "gx"),
        ),
        out_specs=(
            P(("grp", "gx"), "gy", None),
            P("grp", None, None),
            P("grp", None, None),
            P("grp", None),
        ),
        check_vma=False,
    )
```

profile of v0, /device:TPU:0, one launch (start us, length us, event | category | flops | bytes accessed | tf_op | source)
XLA Modules:
  0.0 242.6 jit_solution(7582713262238297557)
XLA Ops:
  7.2 6.3 %all-to-all-start = ((bf16[8,4,8,128]{3,2,1,0:T(8,128)(2,1)}), bf16[8,4,8,128]{3,2,1,0:T(8,128)(2,1)S(1)}, u32[]{:S(2)}, u32[]{:S(2)}) async-start(bf16[8,4,8,128]{3,2,1,0:T(8,128)(2,1)} %param.15), calls=%async_computation | async-start | bytes 131072 | tf_op jit(solution)/shard_map/all_to_all | solution.py:124
  13.5 1.1 fusion.242
  23.4 1.3 collective-permute-start.1
  24.8 4.6 %collective-permute-start = (bf16[2,8,1024]{2,1,0:T(8,128)(2,1)S(1)}, bf16[2,8,1024]{2,1,0:T(8,128)(2,1)S(1)}, u32[]{:S(2)}, u32[]{:S(2)}) collective-permute-start(bf16[2,8,1024]{2,1,0:T(8,128)(2,1)S(1)} %slice.631), channel_id=1, source_target_pairs={{0,4},{4,8},{8,12},{1,5},{5,9},{9,13},{2,6},{6,10},{10,14},{3,7},{... | collective-permute-start | bytes 98312 | tf_op jit(solution)/shard_map/ppermute | solution.py:18
  29.8 1.3 fusion
  31.3 1.3 collective-permute-start.3
  32.6 3.0 %collective-permute-start.2 = (bf16[8,2,1024]{2,1,0:T(2,128)(2,1)S(1)}, bf16[8,2,1024]{2,1,0:T(2,128)(2,1)S(1)}, u32[]{:S(2)}, u32[]{:S(2)}) collective-permute-start(bf16[8,2,1024]{2,1,0:T(2,128)(2,1)S(1)} %get-tuple-element.147), channel_id=1, source_target_pairs={{0,1},{1,2},{2,3},{4,5},{5,6},{6,7},{8,9},{9,10},{10,11},{12,13},{... | collective-permute-start | bytes 98312 | tf_op jit(solution)/shard_map/ppermute | solution.py:18
  42.5 1.3 collective-permute-start.5
  44.0 4.6 %collective-permute-start.4 = (bf16[2,8,1024]{2,1,0:T(8,128)(2,1)S(1)}, bf16[2,8,1024]{2,1,0:T(8,128)(2,1)S(1)}, u32[]{:S(2)}, u32[]{:S(2)}) collective-permute-start(bf16[2,8,1024]{2,1,0:T(8,128)(2,1)S(1)} %slice.673), channel_id=1, source_target_pairs={{0,4},{4,8},{8,12},{1,5},{5,9},{9,13},{2,6},{6,10},{10,14},{3,7},{... | collective-permute-start | bytes 98312 | tf_op jit(solution)/shard_map/ppermute | solution.py:18
  50.1 1.3 collective-permute-start.7
  51.4 3.0 %collective-permute-start.6 = (bf16[8,2,1024]{2,1,0:T(2,128)(2,1)S(1)}, bf16[8,2,1024]{2,1,0:T(2,128)(2,1)S(1)}, u32[]{:S(2)}, u32[]{:S(2)}) collective-permute-start(bf16[8,2,1024]{2,1,0:T(2,128)(2,1)S(1)} %get-tuple-element.143), channel_id=1, source_target_pairs={{0,1},{1,2},{2,3},{4,5},{5,6},{6,7},{8,9},{9,10},{10,11},{12,13},{... | collective-permute-start | bytes 98312 | tf_op jit(solution)/shard_map/ppermute | solution.py:18
  54.5 1.3 collective-permute-start.9
  55.8 4.9 %collective-permute-start.8 = (bf16[2,8,2048]{2,1,0:T(8,128)(2,1)S(1)}, bf16[2,8,2048]{2,1,0:T(8,128)(2,1)S(1)}, u32[]{:S(2)}, u32[]{:S(2)}) collective-permute-start(bf16[2,8,2048]{2,1,0:T(8,128)(2,1)S(1)} %get-tuple-element.141), channel_id=1, source_target_pairs={{0,4},{4,8},{8,12},{1,5},{5,9},{9,13},{2,6},{6,10},{10,14},{3,7},{... | collective-permute-start | bytes 196616 | tf_op jit(solution)/shard_map/ppermute | solution.py:18
  62.7 1.3 collective-permute-start.11
  64.0 5.2 %collective-permute-start.10 = (bf16[8,2,2048]{2,1,0:T(2,128)(2,1)S(1)}, bf16[8,2,2048]{2,1,0:T(2,128)(2,1)S(1)}, u32[]{:S(2)}, u32[]{:S(2)}) collective-permute-start(bf16[8,2,2048]{2,1,0:T(2,128)(2,1)S(1)} %get-tuple-element.139), channel_id=1, source_target_pairs={{0,1},{1,2},{2,3},{4,5},{5,6},{6,7},{8,9},{9,10},{10,11},{12,13},{... | collective-permute-start | bytes 196616 | tf_op jit(solution)/shard_map/ppermute | solution.py:18
  70.1 1.0 convolution_add_fusion.5
  73.8 1.6 pad_slice_fusion.19
  75.4 1.1 fusion.245
  76.8 1.6 pad_slice_fusion.1
  78.4 1.1 fusion.244
  79.5 0.9 copy-done.43
  80.4 0.9 copy-done.42
  81.3 0.9 copy-done.36
  82.2 0.9 copy-done.41
  83.1 0.9 copy-done.34
  84.0 0.9 copy-done.33
  84.9 0.9 copy-done.40
  85.8 0.9 copy-done.31
  86.7 0.9 copy-done.30
  87.6 0.9 copy-done.39
  88.5 0.9 copy-done.29
  89.4 0.9 copy-done.28
  90.3 0.9 copy-done.37
  91.2 0.9 copy-done.27
  92.1 0.9 copy-done.26
  93.0 0.9 copy-done.35
  93.9 0.9 copy-done.25
  94.8 0.9 copy-done.24
  95.7 0.9 copy-done.32
  96.7 0.9 copy-done.23
  97.6 0.9 copy-done.22
  98.5 0.9 copy-done.21
  99.4 0.9 copy-done.20
  100.3 0.9 copy-done.19
  104.6 1.2 copy.159
  105.8 0.9 copy.163
  106.8 0.9 copy-done.17
  107.7 0.9 copy-done.12
  108.6 0.9 copy-done.16
  109.5 0.9 copy-done.10
  110.4 0.9 copy-done.9
  111.3 0.9 copy-done.15
  112.2 0.9 copy-done.7
  113.1 0.9 copy-done.6
  114.0 0.9 copy-done.14
  114.9 0.9 copy-done.5
  115.8 0.9 copy-done.4
  116.8 0.9 copy-done.13
  117.7 0.9 copy-done.3
  124.3 1.2 copy.188
  131.5 99.4 %all-reduce.7.cloned.1.call-done = (f32[27,64,64]{2,1,0:T(8,128)}, f32[27,64,64]{2,1,0:T(8,128)}, f32[512,512]{1,0:T(8,128)}) async-done(((f32[27,64,64]{2,1,0:T(8,128)}, f32[27,64,64]{2,1,0:T(8,128)}, f32[512,512]{1,0:T(8,128)}), (f32[27,64,64]{2,1,0:T(8,128)}, f32[27,64,64]{2,1,0:T(8,128)}, f32[512,512]{1,0:T(8,128)})) %all-reduce.7.cloned.1.call-update) | async-done | bytes 1933328 | tf_op jit(solution)/shard_map/psum | solution.py:173
  230.9 2.3 copy.215
  233.2 0.9 copy.216
  234.7 1.0 copy.217
  (317 shorter events, 39.4 us)
Async XLA Ops:
  7.2 14.5 %all-to-all-start = ((bf16[8,4,8,128]{3,2,1,0:T(8,128)(2,1)}), bf16[8,4,8,128]{3,2,1,0:T(8,128)(2,1)S(1)}, u32[]{:S(2)}, u32[]{:S(2)}) async-start(bf16[8,4,8,128]{3,2,1,0:T(8,128)(2,1)} %param.15), calls=%async_computation | async-start | bytes 131072 | tf_op jit(solution)/shard_map/all_to_all | solution.py:124
  13.5 217.4 %all-reduce.7.cloned.1.call-start = ((), (), s32[]{:S(2)}) async-start(), calls=%async_computation.1 | async-start | bytes 5636096 | tf_op jit(solution)/shard_map/psum | solution.py:173
  13.5 1.2 copy-start.45
  14.7 1.0 copy-start.44
  23.4 7.8 %collective-permute-start.1 = (bf16[2,8,1024]{2,1,0:T(8,128)(2,1)S(1)}, bf16[2,8,1024]{2,1,0:T(8,128)(2,1)S(1)}, u32[]{:S(2)}, u32[]{:S(2)}) collective-permute-start(bf16[2,8,1024]{2,1,0:T(8,128)(2,1)S(1)} %slice.633), channel_id=1, source_target_pairs={{4,0},{8,4},{12,8},{5,1},{9,5},{13,9},{6,2},{10,6},{14,10},{7,3},{... | collective-permute-start | bytes 98312 | tf_op jit(solution)/shard_map/ppermute | solution.py:20
  24.8 6.4 %collective-permute-start = (bf16[2,8,1024]{2,1,0:T(8,128)(2,1)S(1)}, bf16[2,8,1024]{2,1,0:T(8,128)(2,1)S(1)}, u32[]{:S(2)}, u32[]{:S(2)}) collective-permute-start(bf16[2,8,1024]{2,1,0:T(8,128)(2,1)S(1)} %slice.631), channel_id=1, source_target_pairs={{0,4},{4,8},{8,12},{1,5},{5,9},{9,13},{2,6},{6,10},{10,14},{3,7},{... | collective-permute-start | bytes 98312 | tf_op jit(solution)/shard_map/ppermute | solution.py:18
  31.3 5.0 %collective-permute-start.3 = (bf16[8,2,1024]{2,1,0:T(2,128)(2,1)S(1)}, bf16[8,2,1024]{2,1,0:T(2,128)(2,1)S(1)}, u32[]{:S(2)}, u32[]{:S(2)}) collective-permute-start(bf16[8,2,1024]{2,1,0:T(2,128)(2,1)S(1)} %get-tuple-element.148), channel_id=1, source_target_pairs={{1,0},{2,1},{3,2},{5,4},{6,5},{7,6},{9,8},{10,9},{11,10},{13,12},{... | collective-permute-start | bytes 98312 | tf_op jit(solution)/shard_map/ppermute | solution.py:20
  32.6 3.9 %collective-permute-start.2 = (bf16[8,2,1024]{2,1,0:T(2,128)(2,1)S(1)}, bf16[8,2,1024]{2,1,0:T(2,128)(2,1)S(1)}, u32[]{:S(2)}, u32[]{:S(2)}) collective-permute-start(bf16[8,2,1024]{2,1,0:T(2,128)(2,1)S(1)} %get-tuple-element.147), channel_id=1, source_target_pairs={{0,1},{1,2},{2,3},{4,5},{5,6},{6,7},{8,9},{9,10},{10,11},{12,13},{... | collective-permute-start | bytes 98312 | tf_op jit(solution)/shard_map/ppermute | solution.py:18
  42.5 6.8 %collective-permute-start.5 = (bf16[2,8,1024]{2,1,0:T(8,128)(2,1)S(1)}, bf16[2,8,1024]{2,1,0:T(8,128)(2,1)S(1)}, u32[]{:S(2)}, u32[]{:S(2)}) collective-permute-start(bf16[2,8,1024]{2,1,0:T(8,128)(2,1)S(1)} %slice.675), channel_id=1, source_target_pairs={{4,0},{8,4},{12,8},{5,1},{9,5},{13,9},{6,2},{10,6},{14,10},{7,3},{... | collective-permute-start | bytes 98312 | tf_op jit(solution)/shard_map/ppermute | solution.py:20
  44.0 6.1 %collective-permute-start.4 = (bf16[2,8,1024]{2,1,0:T(8,128)(2,1)S(1)}, bf16[2,8,1024]{2,1,0:T(8,128)(2,1)S(1)}, u32[]{:S(2)}, u32[]{:S(2)}) collective-permute-start(bf16[2,8,1024]{2,1,0:T(8,128)(2,1)S(1)} %slice.673), channel_id=1, source_target_pairs={{0,4},{4,8},{8,12},{1,5},{5,9},{9,13},{2,6},{6,10},{10,14},{3,7},{... | collective-permute-start | bytes 98312 | tf_op jit(solution)/shard_map/ppermute | solution.py:18
  50.1 4.4 %copy-start.2 = (bf16[4,8,1024]{2,1,0:T(8,128)(2,1)S(1)}, bf16[4,8,1024]{2,1,0:T(8,128)(2,1)}, u32[]{:S(2)}) copy-start(bf16[4,8,1024]{2,1,0:T(8,128)(2,1)} %param.8) | copy-start | bytes 196612
  50.1 10.6 %collective-permute-start.7 = (bf16[8,2,1024]{2,1,0:T(2,128)(2,1)S(1)}, bf16[8,2,1024]{2,1,0:T(2,128)(2,1)S(1)}, u32[]{:S(2)}, u32[]{:S(2)}) collective-permute-start(bf16[8,2,1024]{2,1,0:T(2,128)(2,1)S(1)} %get-tuple-element.144), channel_id=1, source_target_pairs={{1,0},{2,1},{3,2},{5,4},{6,5},{7,6},{9,8},{10,9},{11,10},{13,12},{... | collective-permute-start | bytes 98312 | tf_op jit(solution)/shard_map/ppermute | solution.py:20
  51.4 9.3 %collective-permute-start.6 = (bf16[8,2,1024]{2,1,0:T(2,128)(2,1)S(1)}, bf16[8,2,1024]{2,1,0:T(2,128)(2,1)S(1)}, u32[]{:S(2)}, u32[]{:S(2)}) collective-permute-start(bf16[8,2,1024]{2,1,0:T(2,128)(2,1)S(1)} %get-tuple-element.143), channel_id=1, source_target_pairs={{0,1},{1,2},{2,3},{4,5},{5,6},{6,7},{8,9},{9,10},{10,11},{12,13},{... | collective-permute-start | bytes 98312 | tf_op jit(solution)/shard_map/ppermute | solution.py:18
  54.5 7.8 %collective-permute-start.9 = (bf16[2,8,2048]{2,1,0:T(8,128)(2,1)S(1)}, bf16[2,8,2048]{2,1,0:T(8,128)(2,1)S(1)}, u32[]{:S(2)}, u32[]{:S(2)}) collective-permute-start(bf16[2,8,2048]{2,1,0:T(8,128)(2,1)S(1)} %get-tuple-element.142), channel_id=1, source_target_pairs={{4,0},{8,4},{12,8},{5,1},{9,5},{13,9},{6,2},{10,6},{14,10},{7,3},{... | collective-permute-start | bytes 196616 | tf_op jit(solution)/shard_map/ppermute | solution.py:20
  55.8 6.8 %collective-permute-start.8 = (bf16[2,8,2048]{2,1,0:T(8,128)(2,1)S(1)}, bf16[2,8,2048]{2,1,0:T(8,128)(2,1)S(1)}, u32[]{:S(2)}, u32[]{:S(2)}) collective-permute-start(bf16[2,8,2048]{2,1,0:T(8,128)(2,1)S(1)} %get-tuple-element.141), channel_id=1, source_target_pairs={{0,4},{4,8},{8,12},{1,5},{5,9},{9,13},{2,6},{6,10},{10,14},{3,7},{... | collective-permute-start | bytes 196616 | tf_op jit(solution)/shard_map/ppermute | solution.py:18
  62.7 10.4 %collective-permute-start.11 = (bf16[8,2,2048]{2,1,0:T(2,128)(2,1)S(1)}, bf16[8,2,2048]{2,1,0:T(2,128)(2,1)S(1)}, u32[]{:S(2)}, u32[]{:S(2)}) collective-permute-start(bf16[8,2,2048]{2,1,0:T(2,128)(2,1)S(1)} %get-tuple-element.140), channel_id=1, source_target_pairs={{1,0},{2,1},{3,2},{5,4},{6,5},{7,6},{9,8},{10,9},{11,10},{13,12},{... | collective-permute-start | bytes 196616 | tf_op jit(solution)/shard_map/ppermute | solution.py:20
  64.0 9.1 %collective-permute-start.10 = (bf16[8,2,2048]{2,1,0:T(2,128)(2,1)S(1)}, bf16[8,2,2048]{2,1,0:T(2,128)(2,1)S(1)}, u32[]{:S(2)}, u32[]{:S(2)}) collective-permute-start(bf16[8,2,2048]{2,1,0:T(2,128)(2,1)S(1)} %get-tuple-element.139), channel_id=1, source_target_pairs={{0,1},{1,2},{2,3},{4,5},{5,6},{6,7},{8,9},{9,10},{10,11},{12,13},{... | collective-permute-start | bytes 196616 | tf_op jit(solution)/shard_map/ppermute | solution.py:18
  78.4 1.1 copy-start.38
  79.4 0.9 copy-start.43
  80.4 0.9 copy-start.42
  81.3 0.9 copy-start.36
  82.2 0.9 copy-start.41
  83.1 0.9 copy-start.34
  84.0 0.9 copy-start.33
  84.9 0.9 copy-start.40
  85.8 0.9 copy-start.31
  86.7 0.9 copy-start.30
  87.6 0.9 copy-start.39
  88.5 0.9 copy-start.29
  89.4 0.9 copy-start.28
  90.3 0.9 copy-start.37
  91.2 0.9 copy-start.27
  92.1 0.9 copy-start.26
  93.0 0.9 copy-start.35
  93.9 0.9 copy-start.25
  94.8 0.9 copy-start.24
  95.7 0.9 copy-start.32
  96.6 0.9 copy-start.23
  97.5 0.9 copy-start.22
  98.4 0.9 copy-start.21
  99.4 0.9 copy-start.20
  100.3 0.9 copy-start.19
  105.8 1.0 copy-start.18
  106.8 0.9 copy-start.17
  107.7 0.9 copy-start.12
  108.6 0.9 copy-start.16
  109.5 0.9 copy-start.10
  110.4 0.9 copy-start.9
  111.3 0.9 copy-start.15
  112.2 0.9 copy-start.7
  113.1 0.9 copy-start.6
  114.0 0.9 copy-start.14
  116.7 0.9 copy-start.13
  117.6 0.9 copy-start.3
  118.6 0.9 copy-start.11
  119.5 0.9 copy-start.8
  120.5 0.9 copy-start.46
  125.5 0.9 copy-start.47
  125.5 1.0 copy-start.48
  125.5 1.0 copy-start.49
  125.5 1.0 copy-start.57
  125.5 1.1 copy-start.59
  230.9 2.3 copy-start.1
  233.2 1.5 copy-start
  (10 other events, 8.2 us)
Sparse Core Ops, SparseCore 0:
  125.7 105.2 all-reduce.6
where the time goes:
time: 244 us; the launch traced here: 243 us
  waiting for transfers between devices  101 us (41%)
  local copies, waits for them, and re-layouts  72.1 us (30%)
  starting transfers between devices  39.3 us (16%)
  between operations  15.4 us (6%)
  matrix products  12.8 us (5%)
    psum x1, waiting for transfers between devices, body(): grad_w_one = lax.psum(one_term, ('gx', 'gy'))  99.4 us
    unnamed x124, local copies, waits for them, and re-layouts  47.6 us
    ppermute x6, starting transfers between devices, padded(): lax.ppermute(tail, axis, [(i, (i + 1) % count) for i in range(ends)])  25.3 us
    ppermute x6, starting transfers between devices, padded(): lax.ppermute(head, axis, [((i + 1) % count, i) for i in range(ends)])  7.75 us
    slice x58, local copies, waits for them, and re-layouts, weight_terms(): sliding_window[:, :, DILATION_STEP * tap_index:DILATION_STEP * tap_index...  6.75 us
    all_to_all x1, starting transfers between devices, body(): lax.all_to_all(out_grad, 'gx', split_axis=0, concat_axis=3, tiled=True)  6.33 us
    dot_general x18, matrix products, data_terms(): jnp.dot(columns, stacked[x_index * 3 + y_index], preferred_element_type=j...  6.06 us
    slice x20, local copies, waits for them, and re-layouts, data_terms(): stacked[x_index * 3 + y_index]  5.96 us
  transfers between devices with their start and end apart: 14, of which 4 were waited for; matrix products, arithmetic and copies ran while one was open for 7% of the time, Pallas kernels for 0%

commit v1 on v0

--- a/solution.py
+++ b/solution.py
@@ -170,7 +170,7 @@
     )
     grad_w_two = lax.psum(two_term, ("gx", "gy"))
     one_term = weight_terms(in_rim, first_backward) * factor
-    grad_w_one = lax.psum(one_term, ("gx", "gy"))
+    grad_w_one = lax.psum(lax.psum(one_term, "gy"), "gx")
     grad_in = (
         data_terms(one_grad_rim, w_one)
         .astype(jnp.bfloat16)

time: 244 us -> 307 us (1.26)
  waiting for transfers between devices: 101 us -> 167 us
  local copies, waits for them, and re-layouts: 72.1 us -> 69 us
    psum x1 -> x3, waiting for transfers between devices: 99.4 us -> 165 us  [the longest x1 101 us: body(): grad_w_two = lax.psum(two_term, ('gx', 'gy'))]
    unnamed x124 -> x118, local copies, waits for them, and re-layouts: 47.6 us -> 46.6 us
  transfers between devices with their start and end apart: 14 -> 16, of which waited for: 4 -> 6; matrix products, arithmetic and copies ran while one was open for 7% -> 7% of each run, Pallas kernels for 0% -> 0%
where the time goes in v1:
time: 307 us; the launch traced here: 305 us
  waiting for transfers between devices  167 us (54%)
  local copies, waits for them, and re-layouts  69 us (22%)
  starting transfers between devices  39.5 us (13%)
  between operations  15.2 us (5%)
  matrix products  12.8 us (4%)
    psum x1, waiting for transfers between devices, body(): grad_w_two = lax.psum(two_term, ('gx', 'gy'))  101 us
    psum x2, waiting for transfers between devices, body(): grad_w_one = lax.psum(lax.psum(one_term, 'gy'), 'gx')  64.8 us
    unnamed x118, local copies, waits for them, and re-layouts  46.6 us
    ppermute x6, starting transfers between devices, padded(): lax.ppermute(tail, axis, [(i, (i + 1) % count) for i in range(ends)])  25.3 us
    ppermute x6, starting transfers between devices, padded(): lax.ppermute(head, axis, [((i + 1) % count, i) for i in range(ends)])  7.75 us
    all_to_all x1, starting transfers between devices, body(): lax.all_to_all(out_grad, 'gx', split_axis=0, concat_axis=3, tiled=True)  6.33 us
  transfers between devices with their start and end apart: 16, of which 6 were waited for; matrix products, arithmetic and copies ran while one was open for 7% of the time, Pallas kernels for 0%

profile of v1, /device:TPU:0, one launch (start us, length us, event | category | flops | bytes accessed | tf_op | source)
XLA Modules:
  0.0 305.5 jit_solution(9193384686141841954)
XLA Ops:
  7.2 6.3 %all-to-all-start = ((bf16[8,4,8,128]{3,2,1,0:T(8,128)(2,1)}), bf16[8,4,8,128]{3,2,1,0:T(8,128)(2,1)S(1)}, u32[]{:S(2)}, u32[]{:S(2)}) async-start(bf16[8,4,8,128]{3,2,1,0:T(8,128)(2,1)} %param.15), calls=%async_computation | async-start | bytes 131072 | tf_op jit(solution)/shard_map/all_to_all | solution.py:124
  13.5 1.1 fusion.242
  22.2 1.3 collective-permute-start.1
  23.6 4.6 %collective-permute-start = (bf16[2,8,1024]{2,1,0:T(8,128)(2,1)S(1)}, bf16[2,8,1024]{2,1,0:T(8,128)(2,1)S(1)}, u32[]{:S(2)}, u32[]{:S(2)}) collective-permute-start(bf16[2,8,1024]{2,1,0:T(8,128)(2,1)S(1)} %slice.631), channel_id=1, source_target_pairs={{0,4},{4,8},{8,12},{1,5},{5,9},{9,13},{2,6},{6,10},{10,14},{3,7},{... | collective-permute-start | bytes 98312 | tf_op jit(solution)/shard_map/ppermute | solution.py:18
  28.6 1.3 fusion
  30.1 1.3 collective-permute-start.3
  31.4 3.0 collective-permute-start.2
  41.5 1.3 collective-permute-start.5
  42.9 4.6 %collective-permute-start.4 = (bf16[2,8,1024]{2,1,0:T(8,128)(2,1)S(1)}, bf16[2,8,1024]{2,1,0:T(8,128)(2,1)S(1)}, u32[]{:S(2)}, u32[]{:S(2)}) collective-permute-start(bf16[2,8,1024]{2,1,0:T(8,128)(2,1)S(1)} %slice.673), channel_id=1, source_target_pairs={{0,4},{4,8},{8,12},{1,5},{5,9},{9,13},{2,6},{6,10},{10,14},{3,7},{... | collective-permute-start | bytes 98312 | tf_op jit(solution)/shard_map/ppermute | solution.py:18
  47.6 1.4 collective-permute-done.4
  49.1 1.3 collective-permute-start.7
  50.4 3.0 collective-permute-start.6
  53.5 1.3 collective-permute-start.9
  54.8 4.9 %collective-permute-start.8 = (bf16[2,8,2048]{2,1,0:T(8,128)(2,1)S(1)}, bf16[2,8,2048]{2,1,0:T(8,128)(2,1)S(1)}, u32[]{:S(2)}, u32[]{:S(2)}) collective-permute-start(bf16[2,8,2048]{2,1,0:T(8,128)(2,1)S(1)} %get-tuple-element.140), channel_id=1, source_target_pairs={{0,4},{4,8},{8,12},{1,5},{5,9},{9,13},{2,6},{6,10},{10,14},{3,7},{... | collective-permute-start | bytes 196616 | tf_op jit(solution)/shard_map/ppermute | solution.py:18
  61.6 1.3 collective-permute-start.11
  62.9 5.3 %collective-permute-start.10 = (bf16[8,2,2048]{2,1,0:T(2,128)(2,1)S(1)}, bf16[8,2,2048]{2,1,0:T(2,128)(2,1)S(1)}, u32[]{:S(2)}, u32[]{:S(2)}) collective-permute-start(bf16[8,2,2048]{2,1,0:T(2,128)(2,1)S(1)} %get-tuple-element.138), channel_id=1, source_target_pairs={{0,1},{1,2},{2,3},{4,5},{5,6},{6,7},{8,9},{9,10},{10,11},{12,13},{... | collective-permute-start | bytes 196616 | tf_op jit(solution)/shard_map/ppermute | solution.py:18
  69.4 1.0 convolution_add_fusion.4
  73.1 1.6 pad_slice_fusion.19
  74.7 1.1 fusion.245
  76.2 1.5 pad_slice_fusion.1
  77.7 1.0 fusion.244
  78.7 0.9 copy-done.43
  79.7 0.9 copy-done.42
  80.6 0.9 copy-done.36
  81.5 0.9 copy-done.41
  82.4 0.9 copy-done.34
  83.3 0.9 copy-done.33
  84.2 0.9 copy-done.40
  85.1 0.9 copy-done.31
  86.0 0.9 copy-done.30
  86.9 0.9 copy-done.39
  87.8 0.9 copy-done.29
  88.7 0.9 copy-done.28
  89.6 0.9 copy-done.37
  90.5 0.9 copy-done.27
  91.4 0.9 copy-done.26
  92.3 0.9 copy-done.35
  93.2 0.9 copy-done.25
  94.1 0.9 copy-done.24
  95.0 0.9 copy-done.32
  95.9 0.9 copy-done.23
  96.8 0.9 copy-done.22
  97.7 0.9 copy-done.21
  98.7 0.9 copy-done.20
  99.6 0.9 copy-done.19
  100.5 0.9 copy-done.18
  101.4 0.9 copy-done.17
  104.8 1.2 copy.159
  107.0 0.9 copy-done.16
  107.9 0.9 copy-done.15
  108.8 0.9 copy-done.9
  109.7 0.9 copy-done.14
  110.6 0.9 copy-done.7
  111.5 0.9 copy-done.6
  113.3 0.9 copy-done.4
  114.2 0.9 copy-done.3
  115.1 0.9 copy-done.12
  122.4 21.8 %all-reduce.9.cloned.1.call-done = f32[27,64,64]{2,1,0:T(8,128)} async-done(((f32[27,64,64]{2,1,0:T(8,128)}), f32[27,64,64]{2,1,0:T(8,128)}) %all-reduce.9.cloned.1.call-update) | async-done | bytes 442384 | tf_op jit(solution)/shard_map/psum | solution.py:173
  144.6 1.2 copy.188
  150.5 43.0 %all-reduce.11.cloned.1.call-done = f32[27,64,64]{2,1,0:T(8,128)} async-done(((f32[27,64,64]{2,1,0:T(8,128)}), f32[27,64,64]{2,1,0:T(8,128)}) %all-reduce.11.cloned.1.call-update) | async-done | bytes 442384 | tf_op jit(solution)/shard_map/psum | solution.py:173
  193.5 100.7 %all-reduce.13.cloned.1.call-done = (f32[27,64,64]{2,1,0:T(8,128)}, f32[512,512]{1,0:T(8,128)}) async-done(((f32[27,64,64]{2,1,0:T(8,128)}, f32[512,512]{1,0:T(8,128)}), (f32[27,64,64]{2,1,0:T(8,128)}, f32[512,512]{1,0:T(8,128)})) %all-reduce.13.cloned.1.call-update) | async-done | bytes 1490960 | tf_op jit(solution)/shard_map/psum | solution.py:171
  294.2 2.3 copy.216
  296.4 0.9 copy.217
  298.0 1.0 copy.218
  (317 shorter events, 37.7 us)
Async XLA Ops:
  7.2 13.4 %all-to-all-start = ((bf16[8,4,8,128]{3,2,1,0:T(8,128)(2,1)}), bf16[8,4,8,128]{3,2,1,0:T(8,128)(2,1)S(1)}, u32[]{:S(2)}, u32[]{:S(2)}) async-start(bf16[8,4,8,128]{3,2,1,0:T(8,128)(2,1)} %param.15), calls=%async_computation | async-start | bytes 131072 | tf_op jit(solution)/shard_map/all_to_all | solution.py:124
  13.5 130.7 %all-reduce.9.cloned.1.call-start = ((), (), s32[]{:S(2)}) async-start(), calls=%async_computation.1 | async-start | bytes 1769472 | tf_op jit(solution)/shard_map/psum | solution.py:173
  13.5 1.2 copy-start.45
  14.7 1.0 copy-start.44
  22.2 7.8 %collective-permute-start.1 = (bf16[2,8,1024]{2,1,0:T(8,128)(2,1)S(1)}, bf16[2,8,1024]{2,1,0:T(8,128)(2,1)S(1)}, u32[]{:S(2)}, u32[]{:S(2)}) collective-permute-start(bf16[2,8,1024]{2,1,0:T(8,128)(2,1)S(1)} %slice.633), channel_id=1, source_target_pairs={{4,0},{8,4},{12,8},{5,1},{9,5},{13,9},{6,2},{10,6},{14,10},{7,3},{... | collective-permute-start | bytes 98312 | tf_op jit(solution)/shard_map/ppermute | solution.py:20
  23.6 6.4 %collective-permute-start = (bf16[2,8,1024]{2,1,0:T(8,128)(2,1)S(1)}, bf16[2,8,1024]{2,1,0:T(8,128)(2,1)S(1)}, u32[]{:S(2)}, u32[]{:S(2)}) collective-permute-start(bf16[2,8,1024]{2,1,0:T(8,128)(2,1)S(1)} %slice.631), channel_id=1, source_target_pairs={{0,4},{4,8},{8,12},{1,5},{5,9},{9,13},{2,6},{6,10},{10,14},{3,7},{... | collective-permute-start | bytes 98312 | tf_op jit(solution)/shard_map/ppermute | solution.py:18
  30.1 5.0 %collective-permute-start.3 = (bf16[8,2,1024]{2,1,0:T(2,128)(2,1)S(1)}, bf16[8,2,1024]{2,1,0:T(2,128)(2,1)S(1)}, u32[]{:S(2)}, u32[]{:S(2)}) collective-permute-start(bf16[8,2,1024]{2,1,0:T(2,128)(2,1)S(1)} %get-tuple-element.147), channel_id=1, source_target_pairs={{1,0},{2,1},{3,2},{5,4},{6,5},{7,6},{9,8},{10,9},{11,10},{13,12},{... | collective-permute-start | bytes 98312 | tf_op jit(solution)/shard_map/ppermute | solution.py:20
  31.4 3.9 %collective-permute-start.2 = (bf16[8,2,1024]{2,1,0:T(2,128)(2,1)S(1)}, bf16[8,2,1024]{2,1,0:T(2,128)(2,1)S(1)}, u32[]{:S(2)}, u32[]{:S(2)}) collective-permute-start(bf16[8,2,1024]{2,1,0:T(2,128)(2,1)S(1)} %get-tuple-element.146), channel_id=1, source_target_pairs={{0,1},{1,2},{2,3},{4,5},{5,6},{6,7},{8,9},{9,10},{10,11},{12,13},{... | collective-permute-start | bytes 98312 | tf_op jit(solution)/shard_map/ppermute | solution.py:18
  41.5 6.1 %collective-permute-start.5 = (bf16[2,8,1024]{2,1,0:T(8,128)(2,1)S(1)}, bf16[2,8,1024]{2,1,0:T(8,128)(2,1)S(1)}, u32[]{:S(2)}, u32[]{:S(2)}) collective-permute-start(bf16[2,8,1024]{2,1,0:T(8,128)(2,1)S(1)} %slice.675), channel_id=1, source_target_pairs={{4,0},{8,4},{12,8},{5,1},{9,5},{13,9},{6,2},{10,6},{14,10},{7,3},{... | collective-permute-start | bytes 98312 | tf_op jit(solution)/shard_map/ppermute | solution.py:20
  42.9 6.1 %collective-permute-start.4 = (bf16[2,8,1024]{2,1,0:T(8,128)(2,1)S(1)}, bf16[2,8,1024]{2,1,0:T(8,128)(2,1)S(1)}, u32[]{:S(2)}, u32[]{:S(2)}) collective-permute-start(bf16[2,8,1024]{2,1,0:T(8,128)(2,1)S(1)} %slice.673), channel_id=1, source_target_pairs={{0,4},{4,8},{8,12},{1,5},{5,9},{9,13},{2,6},{6,10},{10,14},{3,7},{... | collective-permute-start | bytes 98312 | tf_op jit(solution)/shard_map/ppermute | solution.py:18
  49.0 4.4 %copy-start.2 = (bf16[4,8,1024]{2,1,0:T(8,128)(2,1)S(1)}, bf16[4,8,1024]{2,1,0:T(8,128)(2,1)}, u32[]{:S(2)}) copy-start(bf16[4,8,1024]{2,1,0:T(8,128)(2,1)} %param.8) | copy-start | bytes 196612
  49.1 10.6 %collective-permute-start.7 = (bf16[8,2,1024]{2,1,0:T(2,128)(2,1)S(1)}, bf16[8,2,1024]{2,1,0:T(2,128)(2,1)S(1)}, u32[]{:S(2)}, u32[]{:S(2)}) collective-permute-start(bf16[8,2,1024]{2,1,0:T(2,128)(2,1)S(1)} %get-tuple-element.143), channel_id=1, source_target_pairs={{1,0},{2,1},{3,2},{5,4},{6,5},{7,6},{9,8},{10,9},{11,10},{13,12},{... | collective-permute-start | bytes 98312 | tf_op jit(solution)/shard_map/ppermute | solution.py:20
  50.4 9.3 %collective-permute-start.6 = (bf16[8,2,1024]{2,1,0:T(2,128)(2,1)S(1)}, bf16[8,2,1024]{2,1,0:T(2,128)(2,1)S(1)}, u32[]{:S(2)}, u32[]{:S(2)}) collective-permute-start(bf16[8,2,1024]{2,1,0:T(2,128)(2,1)S(1)} %get-tuple-element.142), channel_id=1, source_target_pairs={{0,1},{1,2},{2,3},{4,5},{5,6},{6,7},{8,9},{9,10},{10,11},{12,13},{... | collective-permute-start | bytes 98312 | tf_op jit(solution)/shard_map/ppermute | solution.py:18
  53.5 7.8 %collective-permute-start.9 = (bf16[2,8,2048]{2,1,0:T(8,128)(2,1)S(1)}, bf16[2,8,2048]{2,1,0:T(8,128)(2,1)S(1)}, u32[]{:S(2)}, u32[]{:S(2)}) collective-permute-start(bf16[2,8,2048]{2,1,0:T(8,128)(2,1)S(1)} %get-tuple-element.141), channel_id=1, source_target_pairs={{4,0},{8,4},{12,8},{5,1},{9,5},{13,9},{6,2},{10,6},{14,10},{7,3},{... | collective-permute-start | bytes 196616 | tf_op jit(solution)/shard_map/ppermute | solution.py:20
  54.8 6.8 %collective-permute-start.8 = (bf16[2,8,2048]{2,1,0:T(8,128)(2,1)S(1)}, bf16[2,8,2048]{2,1,0:T(8,128)(2,1)S(1)}, u32[]{:S(2)}, u32[]{:S(2)}) collective-permute-start(bf16[2,8,2048]{2,1,0:T(8,128)(2,1)S(1)} %get-tuple-element.140), channel_id=1, source_target_pairs={{0,4},{4,8},{8,12},{1,5},{5,9},{9,13},{2,6},{6,10},{10,14},{3,7},{... | collective-permute-start | bytes 196616 | tf_op jit(solution)/shard_map/ppermute | solution.py:18
  61.6 10.7 %collective-permute-start.11 = (bf16[8,2,2048]{2,1,0:T(2,128)(2,1)S(1)}, bf16[8,2,2048]{2,1,0:T(2,128)(2,1)S(1)}, u32[]{:S(2)}, u32[]{:S(2)}) collective-permute-start(bf16[8,2,2048]{2,1,0:T(2,128)(2,1)S(1)} %get-tuple-element.139), channel_id=1, source_target_pairs={{1,0},{2,1},{3,2},{5,4},{6,5},{7,6},{9,8},{10,9},{11,10},{13,12},{... | collective-permute-start | bytes 196616 | tf_op jit(solution)/shard_map/ppermute | solution.py:20
  62.9 9.4 %collective-permute-start.10 = (bf16[8,2,2048]{2,1,0:T(2,128)(2,1)S(1)}, bf16[8,2,2048]{2,1,0:T(2,128)(2,1)S(1)}, u32[]{:S(2)}, u32[]{:S(2)}) collective-permute-start(bf16[8,2,2048]{2,1,0:T(2,128)(2,1)S(1)} %get-tuple-element.138), channel_id=1, source_target_pairs={{0,1},{1,2},{2,3},{4,5},{5,6},{6,7},{8,9},{9,10},{10,11},{12,13},{... | collective-permute-start | bytes 196616 | tf_op jit(solution)/shard_map/ppermute | solution.py:18
  77.7 1.1 copy-start.38
  78.7 0.9 copy-start.43
  79.6 0.9 copy-start.42
  80.5 0.9 copy-start.36
  81.4 0.9 copy-start.41
  82.4 0.9 copy-start.34
  83.3 0.9 copy-start.33
  84.2 0.9 copy-start.40
  85.1 0.9 copy-start.31
  86.0 0.9 copy-start.30
  86.9 0.9 copy-start.39
  87.8 0.9 copy-start.29
  88.7 0.9 copy-start.28
  89.6 0.9 copy-start.37
  90.5 0.9 copy-start.27
  91.4 0.9 copy-start.26
  92.3 0.9 copy-start.35
  93.2 0.9 copy-start.25
  94.1 0.9 copy-start.24
  95.0 0.9 copy-start.32
  95.9 0.9 copy-start.23
  96.8 0.9 copy-start.22
  97.7 0.9 copy-start.21
  98.6 0.9 copy-start.20
  99.5 0.9 copy-start.19
  100.4 0.9 copy-start.18
  101.4 0.9 copy-start.17
  106.1 0.9 copy-start.11
  106.1 87.4 %all-reduce.11.cloned.1.call-start = ((), (), s32[]{:S(2)}) async-start(), calls=%async_computation.2 | async-start | bytes 1769472 | tf_op jit(solution)/shard_map/psum | solution.py:173
  107.0 0.9 copy-start.16
  108.8 0.9 copy-start.9
  109.7 0.9 copy-start.14
  110.6 0.9 copy-start.7
  113.3 0.9 copy-start.4
  114.2 0.9 copy-start.3
  115.1 0.9 copy-start.12
  116.0 0.9 copy-start.10
  117.0 0.9 copy-start.8
  117.9 0.9 copy-start.5
  119.0 0.9 copy-start.46
  144.2 150.0 %all-reduce.13.cloned.1.call-start = ((), (), s32[]{:S(2)}) async-start(), calls=%async_computation.3 | async-start | bytes 3866624 | tf_op jit(solution)/shard_map/psum | solution.py:171
  145.8 1.0 copy-start.48
  145.8 1.0 copy-start.49
  145.8 1.0 copy-start.54
  145.8 1.1 copy-start.56
  294.2 2.3 copy-start.1
  296.4 1.5 copy-start
  (9 other events, 7.6 us)
Sparse Core Ops, SparseCore 0:
  106.2 37.9 all-reduce.8
  146.5 46.9 all-reduce.10
  197.7 96.4 all-reduce.12
